TPU v7x, 32 devices: a whole 2x2x4 slice. The times are simulated.
32 devices in a mesh: snp: 8 (over z, x), trait: 4 (over y, core).
Axes of the slice: x: 2, y: 2, z: 4, core: 2. Of those that a mesh axis runs over, the one named last changes fastest.
Arguments:
- genotype: bfloat16 [32, 8192], P(None, 'snp'), may hold values from -0.0625 to 0.0625
- targets: bfloat16 [32, 16384], P('snp', 'trait'), may hold values from -6 to 6
- effect_sizes: float32 [8192, 16384], P('snp', 'trait'), may hold values from -6 to 6
- membership: int32 [4, 128, 128], replicated, may hold values from 0 to 1, as said below
- node_weight: float32 [4, 128], replicated, may hold values from 0.03 to 1
Outputs:
- updated: float32 [8192, 16384], P('snp', 'trait')
Inputs may be any that keep to these rules, and one draw needn't show every extreme that they name: `membership`: at each level the node slots 0 .. c - 1 partition all 128 trait blocks, the remaining slots cover none; every node of a level lies inside one node of the next level; at level 0 each block is its own node.
All inputs are finite; a program needn't handle non-finite values.
Results may differ from a plain program's by a relative error of at most 0.00042.
Values may be sent and summed in bfloat16 or wider, within the bound.
A program may use at most 128 MiB of HBM per device.

v0:
```python
import jax
import jax.numpy as jnp
from jax import lax
from jax.sharding import PartitionSpec as P

TB = 128
LEVELS = 4
step_size = 0.5


def factor_of(node_sq, threshold):
    norm = jnp.sqrt(node_sq)
    return jnp.maximum(norm - threshold, 0.0) / jnp.maximum(norm, threshold)


def shrink_local(value, membership, node_weight):
    local_blocks = value.shape[1] // TB
    first_block = lax.axis_index("trait") * local_blocks
    for level in range(LEVELS):
        member_all = membership[level].astype(jnp.float32)
        count = jnp.sum(member_all, axis=1)
        threshold = step_size * node_weight[level] * jnp.sqrt(TB * jnp.maximum(count, 1.0))
        member = lax.dynamic_slice_in_dim(member_all, first_block, local_blocks, 1)
        blocks = value.reshape(value.shape[0], local_blocks, TB)
        block_sq = jnp.sum(blocks * blocks, axis=2)
        partial_sq = jnp.dot(block_sq, member.T, precision=lax.Precision.HIGHEST)
        node_sq = lax.psum(partial_sq, "trait")
        factor = factor_of(node_sq, threshold)
        block_factor = jnp.dot(factor, member, precision=lax.Precision.HIGHEST)
        value = (blocks * block_factor[:, :, None]).reshape(value.shape)
    return value


def body(genotype, targets, effect_sizes, membership, node_weight):
    current = effect_sizes
    targets_full = lax.all_gather(targets, "snp", axis=0, tiled=True)
    current_bf = current.astype(jnp.bfloat16)
    fitted = lax.psum(jnp.dot(genotype, current_bf, preferred_element_type=jnp.float32), "snp")
    residual = (targets_full.astype(jnp.float32) - fitted).astype(jnp.bfloat16)
    gradient = lax.dot_general(
        genotype, residual, (((0,), (0,)), ((), ())), preferred_element_type=jnp.float32
    )
    current = shrink_local(current + step_size * gradient, membership, node_weight)
    return current


def solution(mesh):
    return jax.shard_map(
        body,
        mesh=mesh,
        in_specs=(P(None, "snp"), P("snp", "trait"), P("snp", "trait"), P(), P()),
        out_specs=P("snp", "trait"),
        check_vma=False,
    )
```

profile of v0, /device:TPU:0, one launch (start us, length us, event | category | flops | bytes accessed | tf_op | source)
XLA Modules:
  0.0 313.8 jit_solution(9431012328404320103)
XLA Ops:
  6.5 0.0 copy-start
  6.5 0.0 all-reduce.6.cloned.1.call-start
  6.5 0.8 copy-done
  7.4 8.1 %fusion = f32[32,4096]{1,0:T(8,128)} fusion(bf16[32,1024]{1,0:T(8,128)(2,1)S(1)} %copy-done, f32[1024,4096]{1,0:T(8,128)} %param.7), kind=kOutput, calls=%fused_computation.9 | convolution fusion | flops 272629760 | bytes 17367040 | tf_op jit(solution)/shard_map/dot_general | solution.py:38
  15.5 0.0 all-reduce.6.cloned.1.call-update
  15.5 0.0 all-reduce.8.cloned.1.call-start
  15.6 0.0 copy-start.3
  15.6 0.0 copy-start.2
  15.6 17.5 %copy.8 = f32[1024,4096]{0,1:T(8,128)} copy(f32[1024,4096]{1,0:T(8,128)} %param.7) | data formatting | bytes 33554432 | tf_op args[2]
  33.1 0.0 copy-done.3
  33.1 32.6 %all-gather = bf16[8,4,4096]{2,1,0:T(4,128)(2,1)S(1)} all-gather(bf16[1,4,4096]{2,1,0:T(4,128)(2,1)S(1)} %bitcast.72), channel_id=1, replica_groups=mesh['snp'=8,'trait'=4] {'snp'}, dimensions={0}, use_global_device_ids=true | all-gather | bytes 294912 | tf_op jit(solution)/shard_map/all_gather | solution.py:36
  65.8 0.0 copy-done.2
  65.8 0.0 copy-start.4
  65.8 25.0 %all-reduce.6.cloned.1.call-done = f32[32,4096]{1,0:T(8,128)} async-done(((f32[32,4096]{1,0:T(8,128)}), f32[32,4096]{1,0:T(8,128)}) %all-reduce.6.cloned.1.call-update) | async-done | bytes 524304 | tf_op jit(solution)/shard_map/psum | solution.py:38
  90.8 11.0 %multiply_reduce_fusion.3 = (f32[1024,32]{0,1:T(8,128)S(1)}, f32[1024,4096]{0,1:T(8,128)}) fusion(f32[1024,4096]{0,1:T(8,128)} %copy.8, bf16[32,1024]{1,0:T(8,128)(2,1)S(1)} %copy-done, f32[32,4096]{1,0:T(8,128)S(1)} %reshape.95, f32[32,4096]{1,0:T(8,128)} %all-reduce.6.cloned.1.call-done), kind=kOutput, calls=%fused_computation.8 | convolution fusion | flops 285442048 | bytes 34799616 | tf_op jit(solution)/shard_map/dot_general | solution.py:40
  101.8 1.8 fusion.24
  103.7 0.0 all-reduce.8.cloned.1.call-update
  103.7 0.0 all-reduce.10.cloned.1.call-start
  103.8 0.1 fusion.53
  103.9 0.0 copy-done.4
  103.9 32.4 %all-reduce.8.cloned.1.call-done = f32[1024,128]{1,0:T(8,128)} async-done(((f32[1024,128]{1,0:T(8,128)}), f32[1024,128]{1,0:T(8,128)}) %all-reduce.8.cloned.1.call-update) | async-done | bytes 524304 | tf_op jit(solution)/shard_map/psum | solution.py:27
  136.3 1.8 fusion.2
  138.2 8.5 %multiply_reduce_fusion.2 = f32[1024,32]{0,1:T(8,128)S(1)} fusion(f32[1024,4096]{0,1:T(8,128)} %get-tuple-element.18, f32[1024,32]{0,1:T(8,128)S(1)} %fusion.2), kind=kLoop, calls=%fused_computation.7 | loop fusion | flops 12550144 | bytes 17039360 | tf_op jit(solution)/shard_map/reduce_sum | solution.py:25
  146.7 1.9 fusion.21
  148.5 0.0 all-reduce.10.cloned.1.call-update
  148.6 0.2 all-reduce.12.cloned.1.call-start
  148.8 33.1 %all-reduce.10.cloned.1.call-done = f32[1024,128]{1,0:T(8,128)} async-done(((f32[1024,128]{1,0:T(8,128)}), f32[1024,128]{1,0:T(8,128)}) %all-reduce.10.cloned.1.call-update) | async-done | bytes 524304 | tf_op jit(solution)/shard_map/psum | solution.py:27
  181.9 1.8 fusion.3
  183.7 9.5 %multiply_reduce_fusion.1 = f32[1024,32]{0,1:T(8,128)S(1)} fusion(f32[1024,4096]{0,1:T(8,128)} %get-tuple-element.18, f32[1024,32]{0,1:T(8,128)S(1)} %fusion.3, f32[1024,32]{0,1:T(8,128)S(1)} %fusion.2), kind=kLoop, calls=%fused_computation.6 | loop fusion | flops 16744448 | bytes 17170432 | tf_op jit(solution)/shard_map/reduce_sum | solution.py:25
  193.2 1.9 fusion.18
  195.1 0.0 all-reduce.12.cloned.1.call-update
  195.1 0.3 all-reduce.14.cloned.1.call-start
  195.4 33.1 %all-reduce.12.cloned.1.call-done = f32[1024,128]{1,0:T(8,128)} async-done(((f32[1024,128]{1,0:T(8,128)}), f32[1024,128]{1,0:T(8,128)}) %all-reduce.12.cloned.1.call-update) | async-done | bytes 524304 | tf_op jit(solution)/shard_map/psum | solution.py:27
  228.4 1.8 fusion.4
  230.2 10.6 %multiply_reduce_fusion = f32[1024,32]{0,1:T(8,128)S(1)} fusion(f32[1024,4096]{0,1:T(8,128)} %get-tuple-element.18, f32[1024,32]{0,1:T(8,128)S(1)} %fusion.4, f32[1024,32]{0,1:T(8,128)S(1)} %fusion.3, f32[1024,32]{0,1:T(8,128)S(1)} %fusion.2), kind=kLoop, calls=%fused_computation.5 | loop fusion | flops 20938752 | bytes 17301504 | tf_op jit(solution)/shard_map/reduce_sum | solution.py:25
  240.8 1.9 fusion.15
  242.7 0.0 all-reduce.14.cloned.1.call-update
  242.7 33.3 %all-reduce.14.cloned.1.call-done = f32[1024,128]{1,0:T(8,128)} async-done(((f32[1024,128]{1,0:T(8,128)}), f32[1024,128]{1,0:T(8,128)}) %all-reduce.14.cloned.1.call-update) | async-done | bytes 524304 | tf_op jit(solution)/shard_map/psum | solution.py:27
  276.0 1.8 fusion.5
  277.9 0.0 copy-start.1
  277.9 12.0 %bitcast_multiply_fusion = f32[1024,4096]{0,1:T(8,128)} fusion(f32[1024,4096]{0,1:T(8,128)} %get-tuple-element.18, f32[1024,32]{0,1:T(8,128)S(1)} %fusion.5, f32[1024,32]{0,1:T(8,128)S(1)} %fusion.4, f32[1024,32]{0,1:T(8,128)S(1)} %fusion.3, f32[1024,32]{0,1:T(8,128)S(1)} %fusion.2), kind=kLoop, calls=%fused_computation | loop fusion | flops 16777216 | bytes 34078720 | tf_op jit(solution)/shard_map/mul | solution.py:30
  289.9 17.4 %copy.9 = f32[1024,4096]{1,0:T(8,128)} copy(f32[1024,4096]{0,1:T(8,128)} %bitcast_multiply_fusion) | data formatting | bytes 33554432 | tf_op jit(solution)/shard_map/mul | solution.py:30
  307.3 0.0 copy-done.1
  (3 shorter events, 0.1 us)
Async XLA Ops:
  6.5 0.8 copy-start
  6.5 84.3 %all-reduce.6.cloned.1.call-start = ((), (), s32[]{:S(2)}) async-start(), calls=%async_computation | async-start | bytes 1048576 | tf_op jit(solution)/shard_map/psum | solution.py:38
  15.5 120.8 %all-reduce.8.cloned.1.call-start = ((), (), s32[]{:S(2)}) async-start(), calls=%async_computation.1 | async-start | bytes 1048576 | tf_op jit(solution)/shard_map/psum | solution.py:27
  15.6 17.5 %copy-start.3 = (bf16[4,4096]{1,0:T(4,128)(2,1)S(1)}, bf16[4,4096]{1,0:T(4,128)(2,1)}, u32[]{:S(2)}) copy-start(bf16[4,4096]{1,0:T(4,128)(2,1)} %param.6) | copy-start | bytes 98308
  15.6 50.2 %copy-start.2 = (s32[4,128,128]{2,1,0:T(8,128)S(1)}, s32[4,128,128]{2,1,0:T(8,128)}, u32[]{:S(2)}) copy-start(s32[4,128,128]{2,1,0:T(8,128)} %param.8) | copy-start | bytes 786436
  65.8 38.1 %copy-start.4 = (f32[4,128]{1,0:T(4,128)S(1)}, f32[4,128]{1,0:T(4,128)}, u32[]{:S(2)}) copy-start(f32[4,128]{1,0:T(4,128)} %param.9) | copy-start | bytes 6148
  103.7 78.2 %all-reduce.10.cloned.1.call-start = ((), (), s32[]{:S(2)}) async-start(), calls=%async_computation.2 | async-start | bytes 1048576 | tf_op jit(solution)/shard_map/psum | solution.py:27
  148.6 79.8 %all-reduce.12.cloned.1.call-start = ((), (), s32[]{:S(2)}) async-start(), calls=%async_computation.3 | async-start | bytes 1048576 | tf_op jit(solution)/shard_map/psum | solution.py:27
  195.1 80.9 %all-reduce.14.cloned.1.call-start = ((), (), s32[]{:S(2)}) async-start(), calls=%async_computation.4 | async-start | bytes 1048576 | tf_op jit(solution)/shard_map/psum | solution.py:27
  277.9 29.4 %copy-start.1 = (bf16[32,1024]{1,0:T(8,128)(2,1)S(1)}, bf16[32,1024]{1,0:T(8,128)(2,1)}, u32[]{:S(2)}) copy-start(bf16[32,1024]{1,0:T(8,128)(2,1)} %param.5) | copy-start | bytes 196612
Sparse Core Ops, SparseCore 0:
  15.6 75.1 all-reduce.5
  103.8 32.4 all-reduce.7
  148.7 33.1 all-reduce.9
  195.2 33.1 all-reduce.11
  242.8 33.1 all-reduce.13
where the time goes:
time: 315 us; the launch traced here: 314 us
  waiting for transfers between devices  157 us (50%)
  other arithmetic  40.7 us (13%)
  local copies, waits for them, and re-layouts  35.8 us (11%)
  matrix products  33.9 us (11%)
  blocking collectives  32.6 us (10%)
  between operations  13.3 us (4%)
    psum x4, waiting for transfers between devices, shrink_local(): node_sq = lax.psum(partial_sq, 'trait')  132 us
    all_gather x1, blocking collectives, body(): targets_full = lax.all_gather(targets, 'snp', axis=0, tiled=True)  32.6 us
    reduce_sum x3, other arithmetic, shrink_local(): block_sq = jnp.sum(blocks * blocks, axis=2)  28.6 us
    psum x1, waiting for transfers between devices, body(): lax.psum(jnp.dot(genotype, current_bf, preferred_element_type=jnp.float32...  25 us
    unnamed x11, local copies, waits for them, and re-layouts  18.4 us
    mul x1, local copies, waits for them, and re-layouts, shrink_local(): value = (blocks * block_factor[:, :, None]).reshape(value.shape)  17.4 us
    mul x1, other arithmetic, shrink_local(): value = (blocks * block_factor[:, :, None]).reshape(value.shape)  12 us
    dot_general x1, matrix products, body(): lax.dot_general(genotype, residual, (((0,), (0,)), ((), ())), preferred_e...  11 us
  transfers between devices with their start and end apart: 5, of which 5 were waited for; matrix products, arithmetic and copies ran while one was open for 6% of the time, Pallas kernels for 0%

commit v1 on v0

--- a/solution.py
+++ b/solution.py
@@ -6,6 +6,12 @@
 TB = 128
 LEVELS = 4
 step_size = 0.5
+
+
+def joined_along(blocks, dim):
+    blocks = jnp.moveaxis(blocks, 0, dim)
+    shape = blocks.shape
+    return blocks.reshape(*shape[:dim], shape[dim] * shape[dim + 1], *shape[dim + 2 :])
 
 
 def factor_of(node_sq, threshold):
@@ -33,7 +39,19 @@
 
 def body(genotype, targets, effect_sizes, membership, node_weight):
     current = effect_sizes
-    targets_full = lax.all_gather(targets, "snp", axis=0, tiled=True)
+    size = lax.axis_size("snp")
+    pairs = [(i, (i + 1) % size) for i in range(size)]
+    back = [(b, a) for a, b in pairs]
+    lower, upper = ([], [])
+    for step in range(size - 1):
+        if step % 2 == 0:
+            lower.append(lax.ppermute(lower[-1] if lower else targets, "snp", pairs))
+        else:
+            upper.append(lax.ppermute(upper[-1] if upper else targets, "snp", back))
+    pieces = jnp.stack([*lower[::-1], targets, *upper])
+    shift = lax.axis_index("snp") - len(lower)
+    pieces = pieces[(jnp.arange(size) - shift) % size]
+    targets_full = joined_along(pieces, 0)
     current_bf = current.astype(jnp.bfloat16)
     fitted = lax.psum(jnp.dot(genotype, current_bf, preferred_element_type=jnp.float32), "snp")
     residual = (targets_full.astype(jnp.float32) - fitted).astype(jnp.bfloat16)

time: 315 us -> 316 us (level)
  blocking collectives: 32.6 us -> 0 us
  waiting for transfers between devices: 157 us -> 176 us
  starting transfers between devices: 0.57 us -> 16.1 us
    all_gather x1 -> x0, blocking collectives: 32.6 us -> none  [body(): targets_full = lax.all_gather(targets, 'snp', axis=0, tiled=True)]
    ppermute x0 -> x7, starting transfers between devices: none -> 15.6 us  [the longest x3 12.6 us: body(): upper.append(lax.ppermute(upper[-1] if upper else targets, 'snp', back))]
    ppermute x0 -> x7, waiting for transfers between devices: none -> 10.2 us  [the longest x4 8.78 us: body(): lower.append(lax.ppermute(lower[-1] if lower else targets, 'snp', pairs))]
    psum x1, waiting for transfers between devices: 25 us -> 33.4 us  [body(): lax.psum(jnp.dot(genotype, current_bf, preferred_element_type=jnp.float32...]
    unnamed x11 -> x18, local copies, waits for them, and re-layouts: 18.4 us -> 17.7 us
  transfers between devices with their start and end apart: 5 -> 12, of which waited for: 5 -> 8; matrix products, arithmetic and copies ran while one was open for 6% -> 8% of each run, Pallas kernels for 0% -> 0%
where the time goes in v1:
time: 316 us
  waiting for transfers between devices  176 us (56%)
  other arithmetic  40.8 us (13%)
  local copies, waits for them, and re-layouts  35.9 us (11%)
  matrix products  33.9 us (11%)
  starting transfers between devices  16.1 us (5%)
  between operations  13.3 us (4%)
    psum x4, waiting for transfers between devices, shrink_local(): node_sq = lax.psum(partial_sq, 'trait')  132 us
    psum x1, waiting for transfers between devices, body(): lax.psum(jnp.dot(genotype, current_bf, preferred_element_type=jnp.float32...  33.4 us
    reduce_sum x3, other arithmetic, shrink_local(): block_sq = jnp.sum(blocks * blocks, axis=2)  28.6 us
    unnamed x18, local copies, waits for them, and re-layouts  17.7 us
    mul x1, local copies, waits for them, and re-layouts, shrink_local(): value = (blocks * block_factor[:, :, None]).reshape(value.shape)  17.4 us
    ppermute x3, starting transfers between devices, body(): upper.append(lax.ppermute(upper[-1] if upper else targets, 'snp', back))  12.6 us
    mul x1, other arithmetic, shrink_local(): value = (blocks * block_factor[:, :, None]).reshape(value.shape)  12 us
    dot_general x1, matrix products, body(): lax.dot_general(genotype, residual, (((0,), (0,)), ((), ())), preferred_e...  11 us
  transfers between devices with their start and end apart: 12, of which 8 were waited for; matrix products, arithmetic and copies ran while one was open for 8% of the time, Pallas kernels for 0%

profile of v1, /device:TPU:0, one launch (start us, length us, event | category | flops | bytes accessed | tf_op | source)
XLA Modules:
  0.0 315.6 jit_solution(14824154680079157013)
XLA Ops:
  6.5 2.9 collective-permute-start
  9.5 3.1 collective-permute-start.4
  12.6 8.1 %fusion = f32[32,4096]{1,0:T(8,128)} fusion(bf16[32,1024]{1,0:T(8,128)(2,1)S(1)} %copy-done, f32[1024,4096]{1,0:T(8,128)} %param.7), kind=kOutput, calls=%fused_computation.10 | convolution fusion | flops 272629760 | bytes 17367040 | tf_op jit(solution)/shard_map/dot_general | solution.py:56
  20.7 0.0 all-reduce.6.cloned.1.call-update
  20.7 0.0 all-reduce.8.cloned.1.call-start
  20.8 0.0 collective-permute-done
  20.8 0.1 collective-permute-start.1
  20.9 6.7 %collective-permute-done.1 = bf16[4,4096]{1,0:T(4,128)(2,1)S(1)} collective-permute-done((bf16[4,4096]{1,0:T(4,128)(2,1)S(1)}, bf16[4,4096]{1,0:T(4,128)(2,1)S(1)}, u32[]{:S(2)}, u32[]{:S(2)}) %collective-permute-start.1) | collective-permute-done | bytes 32800 | tf_op jit(solution)/shard_map/ppermute | solution.py:48
  27.6 0.0 collective-permute-start.2
  27.6 0.0 collective-permute-done.4
  27.6 4.8 %collective-permute-start.5 = (bf16[4,4096]{1,0:T(4,128)(2,1)S(1)}, bf16[4,4096]{1,0:T(4,128)(2,1)S(1)}, u32[]{:S(2)}, u32[]{:S(2)}) collective-permute-start(bf16[4,4096]{1,0:T(4,128)(2,1)S(1)} %collective-permute-done.4), channel_id=1, source_target_pairs={{4,0},{8,4},{12,8},{16,12},{20,16},{24,20},{28,24},{0,28},{5,1},{9... | collective-permute-start | bytes 98312 | tf_op jit(solution)/shard_map/ppermute | solution.py:50
  32.4 2.1 collective-permute-done.2
  34.5 0.0 copy-start.3
  34.5 17.5 %copy.8 = f32[1024,4096]{0,1:T(8,128)} copy(f32[1024,4096]{1,0:T(8,128)} %param.7) | data formatting | bytes 33554432 | tf_op args[2]
  52.0 0.0 collective-permute-done.5
  52.0 4.7 %collective-permute-start.6 = (bf16[4,4096]{1,0:T(4,128)(2,1)S(1)}, bf16[4,4096]{1,0:T(4,128)(2,1)S(1)}, u32[]{:S(2)}, u32[]{:S(2)}) collective-permute-start(bf16[4,4096]{1,0:T(4,128)(2,1)S(1)} %collective-permute-done.5), channel_id=1, source_target_pairs={{4,0},{8,4},{12,8},{16,12},{20,16},{24,20},{28,24},{0,28},{5,1},{9... | collective-permute-start | bytes 98312 | tf_op jit(solution)/shard_map/ppermute | solution.py:50
  56.7 0.0 collective-permute-done.3
  56.9 1.4 collective-permute-done.6
  58.3 0.8 gather_fusion
  59.1 0.0 copy-start.4
  59.2 33.4 %all-reduce.6.cloned.1.call-done = f32[32,4096]{1,0:T(8,128)} async-done(((f32[32,4096]{1,0:T(8,128)}), f32[32,4096]{1,0:T(8,128)}) %all-reduce.6.cloned.1.call-update) | async-done | bytes 524304 | tf_op jit(solution)/shard_map/psum | solution.py:56
  92.5 11.0 %multiply_reduce_fusion.3 = (f32[1024,32]{0,1:T(8,128)S(1)}, f32[1024,4096]{0,1:T(8,128)}) fusion(f32[1024,4096]{0,1:T(8,128)} %copy.8, bf16[32,1024]{1,0:T(8,128)(2,1)S(1)} %copy-done, f32[32,4096]{1,0:T(8,128)S(1)} %reshape.145, f32[32,4096]{1,0:T(8,128)} %all-reduce.6.cloned.1.call-done), kind=kOutput, calls=%fused_computation.9 | convolution fusion | flops 285442048 | bytes 34799616 | tf_op jit(solution)/shard_map/dot_general | solution.py:58
  103.5 1.8 fusion.24
  105.4 0.0 all-reduce.8.cloned.1.call-update
  105.4 0.0 all-reduce.10.cloned.1.call-start
  105.5 0.1 fusion.55
  105.6 32.4 %all-reduce.8.cloned.1.call-done = f32[1024,128]{1,0:T(8,128)} async-done(((f32[1024,128]{1,0:T(8,128)}), f32[1024,128]{1,0:T(8,128)}) %all-reduce.8.cloned.1.call-update) | async-done | bytes 524304 | tf_op jit(solution)/shard_map/psum | solution.py:33
  138.1 1.8 fusion.2
  139.9 8.5 %multiply_reduce_fusion.2 = f32[1024,32]{0,1:T(8,128)S(1)} fusion(f32[1024,4096]{0,1:T(8,128)} %get-tuple-element.18, f32[1024,32]{0,1:T(8,128)S(1)} %fusion.2), kind=kLoop, calls=%fused_computation.8 | loop fusion | flops 12550144 | bytes 17039360 | tf_op jit(solution)/shard_map/reduce_sum | solution.py:31
  148.4 1.9 fusion.21
  150.3 0.0 all-reduce.10.cloned.1.call-update
  150.3 0.2 all-reduce.12.cloned.1.call-start
  150.5 33.1 %all-reduce.10.cloned.1.call-done = f32[1024,128]{1,0:T(8,128)} async-done(((f32[1024,128]{1,0:T(8,128)}), f32[1024,128]{1,0:T(8,128)}) %all-reduce.10.cloned.1.call-update) | async-done | bytes 524304 | tf_op jit(solution)/shard_map/psum | solution.py:33
  183.6 1.8 fusion.3
  185.4 9.5 %multiply_reduce_fusion.1 = f32[1024,32]{0,1:T(8,128)S(1)} fusion(f32[1024,4096]{0,1:T(8,128)} %get-tuple-element.18, f32[1024,32]{0,1:T(8,128)S(1)} %fusion.3, f32[1024,32]{0,1:T(8,128)S(1)} %fusion.2), kind=kLoop, calls=%fused_computation.7 | loop fusion | flops 16744448 | bytes 17170432 | tf_op jit(solution)/shard_map/reduce_sum | solution.py:31
  194.9 1.9 fusion.18
  196.8 0.0 all-reduce.12.cloned.1.call-update
  196.8 0.3 all-reduce.14.cloned.1.call-start
  197.1 33.1 %all-reduce.12.cloned.1.call-done = f32[1024,128]{1,0:T(8,128)} async-done(((f32[1024,128]{1,0:T(8,128)}), f32[1024,128]{1,0:T(8,128)}) %all-reduce.12.cloned.1.call-update) | async-done | bytes 524304 | tf_op jit(solution)/shard_map/psum | solution.py:33
  230.1 1.8 fusion.4
  232.0 10.6 %multiply_reduce_fusion = f32[1024,32]{0,1:T(8,128)S(1)} fusion(f32[1024,4096]{0,1:T(8,128)} %get-tuple-element.18, f32[1024,32]{0,1:T(8,128)S(1)} %fusion.4, f32[1024,32]{0,1:T(8,128)S(1)} %fusion.3, f32[1024,32]{0,1:T(8,128)S(1)} %fusion.2), kind=kLoop, calls=%fused_computation.6 | loop fusion | flops 20938752 | bytes 17301504 | tf_op jit(solution)/shard_map/reduce_sum | solution.py:31
  242.5 1.9 fusion.15
  244.4 0.0 all-reduce.14.cloned.1.call-update
  244.4 33.3 %all-reduce.14.cloned.1.call-done = f32[1024,128]{1,0:T(8,128)} async-done(((f32[1024,128]{1,0:T(8,128)}), f32[1024,128]{1,0:T(8,128)}) %all-reduce.14.cloned.1.call-update) | async-done | bytes 524304 | tf_op jit(solution)/shard_map/psum | solution.py:33
  277.7 1.8 fusion.5
  279.6 0.0 copy-start.1
  279.6 12.0 %bitcast_multiply_fusion = f32[1024,4096]{0,1:T(8,128)} fusion(f32[1024,4096]{0,1:T(8,128)} %get-tuple-element.18, f32[1024,32]{0,1:T(8,128)S(1)} %fusion.5, f32[1024,32]{0,1:T(8,128)S(1)} %fusion.4, f32[1024,32]{0,1:T(8,128)S(1)} %fusion.3, f32[1024,32]{0,1:T(8,128)S(1)} %fusion.2), kind=kLoop, calls=%fused_computation.1 | loop fusion | flops 16777216 | bytes 34078720 | tf_op jit(solution)/shard_map/mul | solution.py:36
  291.6 17.4 %copy.9 = f32[1024,4096]{1,0:T(8,128)} copy(f32[1024,4096]{0,1:T(8,128)} %bitcast_multiply_fusion) | data formatting | bytes 33554432 | tf_op jit(solution)/shard_map/mul | solution.py:36
  (22 shorter events, 0.3 us)
Async XLA Ops:
  6.5 6.0 %copy-start = (bf16[32,1024]{1,0:T(8,128)(2,1)S(1)}, bf16[32,1024]{1,0:T(8,128)(2,1)}, u32[]{:S(2)}) copy-start(bf16[32,1024]{1,0:T(8,128)(2,1)} %param.5) | copy-start | bytes 196612
  6.5 14.3 %copy-start.2 = (s32[4,128,128]{2,1,0:T(8,128)S(1)}, s32[4,128,128]{2,1,0:T(8,128)}, u32[]{:S(2)}) copy-start(s32[4,128,128]{2,1,0:T(8,128)} %param.8) | copy-start | bytes 786436
  6.5 86.0 %all-reduce.6.cloned.1.call-start = ((), (), s32[]{:S(2)}) async-start(), calls=%async_computation | async-start | bytes 1048576 | tf_op jit(solution)/shard_map/psum | solution.py:56
  6.5 14.2 %collective-permute-start = (bf16[4,4096]{1,0:T(4,128)(2,1)}, bf16[4,4096]{1,0:T(4,128)(2,1)S(1)}, u32[]{:S(2)}, u32[]{:S(2)}) collective-permute-start(bf16[4,4096]{1,0:T(4,128)(2,1)} %param.6), channel_id=1, source_target_pairs={{0,4},{4,8},{8,12},{12,16},{16,20},{20,24},{24,28},{28,0},{1,5},{5... | collective-permute-start | bytes 98312 | tf_op jit(solution)/shard_map/ppermute | solution.py:48
  9.5 18.1 %collective-permute-start.4 = (bf16[4,4096]{1,0:T(4,128)(2,1)}, bf16[4,4096]{1,0:T(4,128)(2,1)S(1)}, u32[]{:S(2)}, u32[]{:S(2)}) collective-permute-start(bf16[4,4096]{1,0:T(4,128)(2,1)} %param.6), channel_id=1, source_target_pairs={{4,0},{8,4},{12,8},{16,12},{20,16},{24,20},{28,24},{0,28},{5,1},{9... | collective-permute-start | bytes 98312 | tf_op jit(solution)/shard_map/ppermute | solution.py:50
  20.7 117.3 %all-reduce.8.cloned.1.call-start = ((), (), s32[]{:S(2)}) async-start(), calls=%async_computation.1 | async-start | bytes 1048576 | tf_op jit(solution)/shard_map/psum | solution.py:33
  20.8 6.8 %collective-permute-start.1 = (bf16[4,4096]{1,0:T(4,128)(2,1)S(1)}, bf16[4,4096]{1,0:T(4,128)(2,1)S(1)}, u32[]{:S(2)}, u32[]{:S(2)}) collective-permute-start(bf16[4,4096]{1,0:T(4,128)(2,1)S(1)} %collective-permute-done), channel_id=1, source_target_pairs={{0,4},{4,8},{8,12},{12,16},{16,20},{20,24},{24,28},{28,0},{1,5},{5... | collective-permute-start | bytes 98312 | tf_op jit(solution)/shard_map/ppermute | solution.py:48
  27.6 6.9 %collective-permute-start.2 = (bf16[4,4096]{1,0:T(4,128)(2,1)S(1)}, bf16[4,4096]{1,0:T(4,128)(2,1)S(1)}, u32[]{:S(2)}, u32[]{:S(2)}) collective-permute-start(bf16[4,4096]{1,0:T(4,128)(2,1)S(1)} %collective-permute-done.1), channel_id=1, source_target_pairs={{0,4},{4,8},{8,12},{12,16},{16,20},{20,24},{24,28},{28,0},{1,5},{5... | collective-permute-start | bytes 98312 | tf_op jit(solution)/shard_map/ppermute | solution.py:48
  27.6 24.4 %collective-permute-start.5 = (bf16[4,4096]{1,0:T(4,128)(2,1)S(1)}, bf16[4,4096]{1,0:T(4,128)(2,1)S(1)}, u32[]{:S(2)}, u32[]{:S(2)}) collective-permute-start(bf16[4,4096]{1,0:T(4,128)(2,1)S(1)} %collective-permute-done.4), channel_id=1, source_target_pairs={{4,0},{8,4},{12,8},{16,12},{20,16},{24,20},{28,24},{0,28},{5,1},{9... | collective-permute-start | bytes 98312 | tf_op jit(solution)/shard_map/ppermute | solution.py:50
  34.5 22.2 %collective-permute-start.3 = (bf16[4,4096]{1,0:T(4,128)(2,1)S(1)}, bf16[4,4096]{1,0:T(4,128)(2,1)S(1)}, u32[]{:S(2)}, u32[]{:S(2)}) collective-permute-start(bf16[4,4096]{1,0:T(4,128)(2,1)S(1)} %collective-permute-done.2), channel_id=1, source_target_pairs={{0,4},{4,8},{8,12},{12,16},{16,20},{20,24},{24,28},{28,0},{1,5},{5... | collective-permute-start | bytes 98312 | tf_op jit(solution)/shard_map/ppermute | solution.py:48
  34.5 22.3 %copy-start.3 = (bf16[4,4096]{1,0:T(4,128)(2,1)S(1)}, bf16[4,4096]{1,0:T(4,128)(2,1)}, u32[]{:S(2)}) copy-start(bf16[4,4096]{1,0:T(4,128)(2,1)} %param.6) | copy-start | bytes 98308
  52.0 6.3 %collective-permute-start.6 = (bf16[4,4096]{1,0:T(4,128)(2,1)S(1)}, bf16[4,4096]{1,0:T(4,128)(2,1)S(1)}, u32[]{:S(2)}, u32[]{:S(2)}) collective-permute-start(bf16[4,4096]{1,0:T(4,128)(2,1)S(1)} %collective-permute-done.5), channel_id=1, source_target_pairs={{4,0},{8,4},{12,8},{16,12},{20,16},{24,20},{28,24},{0,28},{5,1},{9... | collective-permute-start | bytes 98312 | tf_op jit(solution)/shard_map/ppermute | solution.py:50
  59.1 46.5 %copy-start.4 = (f32[4,128]{1,0:T(4,128)S(1)}, f32[4,128]{1,0:T(4,128)}, u32[]{:S(2)}) copy-start(f32[4,128]{1,0:T(4,128)} %param.9) | copy-start | bytes 6148
  105.4 78.2 %all-reduce.10.cloned.1.call-start = ((), (), s32[]{:S(2)}) async-start(), calls=%async_computation.2 | async-start | bytes 1048576 | tf_op jit(solution)/shard_map/psum | solution.py:33
  150.3 79.8 %all-reduce.12.cloned.1.call-start = ((), (), s32[]{:S(2)}) async-start(), calls=%async_computation.3 | async-start | bytes 1048576 | tf_op jit(solution)/shard_map/psum | solution.py:33
  196.8 80.9 %all-reduce.14.cloned.1.call-start = ((), (), s32[]{:S(2)}) async-start(), calls=%async_computation.4 | async-start | bytes 1048576 | tf_op jit(solution)/shard_map/psum | solution.py:33
  279.6 29.4 %copy-start.1 = (bf16[32,1024]{1,0:T(8,128)(2,1)S(1)}, bf16[32,1024]{1,0:T(8,128)(2,1)}, u32[]{:S(2)}) copy-start(bf16[32,1024]{1,0:T(8,128)(2,1)} %param.5) | copy-start | bytes 196612
Sparse Core Ops, SparseCore 0:
  20.9 71.6 all-reduce.5
  105.5 32.4 all-reduce.7
  150.4 33.1 all-reduce.9
  196.9 33.1 all-reduce.11
  244.5 33.1 all-reduce.13
